TPU v7x, 512 devices: a whole 4x8x8 slice. The times are simulated.
512 devices in a mesh: dp: 4 (over x), expert: 8 (over y), etp: 16 (over z, core).
Axes of the slice: x: 4, y: 8, z: 8, core: 2. Of those that a mesh axis runs over, the one named last changes fastest.
Arguments:
- tokens: bfloat16 [4096, 3072], P(('dp', 'expert')), parts along dimension 0, may hold values from -6 to 6
- routes: int32 [4096, 2], P(('dp', 'expert')), parts along dimension 0, may hold values from 0 to 3, all different within a row; in each aligned block of 128 rows (0 to 127, 128 to 255, ...) at most 80 rows name the same one
- route_weight: float32 [4096, 2], P(('dp', 'expert')), parts along dimension 0, may hold values from 0.2 to 1
- w_in: bfloat16 [8, 3072, 4096], P('expert', None, 'etp'), may hold values from -0.109375 to 0.109375
- w_out: bfloat16 [8, 4096, 3072], P('expert', 'etp'), may hold values from -0.0625 to 0.0625
Outputs:
- moe_output: bfloat16 [4096, 3072], P(('dp', 'expert')), parts along dimension 0
There are 4 independent parts, one for each index of `dp`. A program takes and returns all parts, laid end to end along the dimension named above; an argument that names none is the same for every part. Nothing has to cross between parts.
Inputs may be any that keep to these rules, and one draw needn't show every extreme that they name: `routes`: each row names two different experts. Within each aligned block of 128 rows (the rows of one index of the expert axis) no expert is named by more than 80 rows, a bound that some block reaches.
All inputs are finite; a program needn't handle non-finite values.
Results may differ from a plain program's by a relative error of at most 0.018.
Values may be sent and summed in bfloat16 or wider, within the bound.
No kernel may reach another device: no remote copies, remote signals or barrier semaphores. Data moves between devices by JAX's collectives and lax.ppermute only.
A program may use at most 64 MiB of HBM per device.

v0:
```python
import jax
import jax.numpy as jnp
from jax import lax
from jax.sharding import PartitionSpec as P


def on_device(tokens, routes, route_weight, w_in, w_out):
    n_index = lax.axis_size("expert")
    n_tensor = lax.axis_size("etp")
    halves = max(1, n_index // 4)
    n_experts = n_index // halves
    tok_rows = tokens.shape[0]
    model_width = tokens.shape[1]
    rounded_up = (2 * tok_rows // n_experts + tok_rows // 8 + n_tensor - 1) // n_tensor * n_tensor
    capacity = min(tok_rows, rounded_up)
    chosen = routes.reshape(-1)
    indicator = (chosen[:, None] == jnp.arange(n_experts, dtype=jnp.int32)[None, :]).astype(
        jnp.int32
    )
    preceding = jnp.cumsum(indicator, axis=0) - indicator
    position = jnp.sum(preceding * indicator, axis=1)
    destination = chosen * capacity + position
    duplicated = jnp.repeat(tokens, 2, axis=0)
    packed = (
        jnp.zeros((n_experts * capacity, model_width), jnp.bfloat16).at[destination].set(duplicated)
    )
    outgoing = jnp.repeat(packed.reshape(n_experts, capacity, model_width), halves, axis=0)
    w_first = w_in[0]
    w_second = w_out[0]
    arrived = lax.all_to_all(outgoing, "expert", split_axis=0, concat_axis=0, tiled=True)
    flat_rows = arrived.reshape(-1, model_width)
    projected = jnp.dot(flat_rows, w_first, preferred_element_type=jnp.float32)
    hidden = jax.nn.silu(projected).astype(jnp.bfloat16)
    term = jnp.dot(hidden, w_second, preferred_element_type=jnp.float32)
    rounded = lax.optimization_barrier(term.astype(jnp.bfloat16))
    partial_terms = rounded.astype(jnp.float32).reshape(arrived.shape[:-1] + (model_width,))
    summed = lax.psum_scatter(
        partial_terms.astype(jnp.bfloat16), "etp", scatter_dimension=1, tiled=True
    ).astype(jnp.float32)
    homeward = lax.all_to_all(
        summed.astype(jnp.bfloat16), "expert", split_axis=0, concat_axis=0, tiled=True
    ).astype(summed.dtype)
    gathered = lax.all_gather(homeward.astype(jnp.bfloat16), "etp", axis=1, tiled=True).astype(
        homeward.dtype
    )
    home_rows = gathered.reshape(n_index * capacity, model_width)
    combined = jnp.zeros((tok_rows * 2, model_width), jnp.float32)
    for half_index in range(halves):
        combined = combined + home_rows[(chosen * halves + half_index) * capacity + position]
    weighted = combined.reshape(tok_rows, 2, model_width) * route_weight[:, :, None]
    return jnp.sum(weighted, axis=1).astype(jnp.bfloat16)


def solution(mesh):
    placed = (
        P(("dp", "expert"), None),
        P(("dp", "expert"), None),
        P(("dp", "expert"), None),
        P("expert", None, "etp"),
        P("expert", "etp", None),
    )
    return jax.shard_map(
        on_device, mesh=mesh, in_specs=placed, out_specs=P(("dp", "expert"), None), check_vma=False
    )
```

profile of v0, /device:TPU:1, one launch (start us, length us, event | category | flops | bytes accessed | tf_op | source)
XLA Modules:
  0.0 307.0 jit_solution(10249326293521199883)
XLA Ops:
  6.5 0.0 copy-start
  6.5 0.0 reduce-scatter.2.cloned.1.call-start
  6.5 0.9 copy.28
  7.4 0.1 eq.29
  7.6 0.1 eq.25
  7.7 0.7 add_multiply_fusion
  8.4 1.2 reduce-window.6
  9.6 0.1 slice.12
  9.7 0.1 copy.30
  9.9 0.1 copy.31
  10.0 0.1 add_bitcast_fusion
  10.0 0.1 copy.27
  10.1 0.1 mul.69
  10.3 0.1 copy.36
  10.4 0.1 mul.74
  10.5 0.1 copy.37
  10.7 0.1 mul.77
  10.8 1.9 broadcast_in_dim.7
  12.8 1.5 reshape.166
  14.3 4.2 %scatter_custom_fusion = bf16[320,3072]{1,0:T(8,128)(2,1)S(1)} fusion(s32[256]{0:T(256)S(1)} %bitcast.49, bf16[256,3072]{1,0:T(8,128)(2,1)} %reshape.166, bf16[]{:T(256)} %constant.5.clone.1), kind=kCustom, calls=%fused_computation.8 | custom fusion | bytes 1966592 | tf_op jit(solution)/shard_map/scatter | solution.py:25
  18.5 0.6 broadcast_in_dim.16
  19.1 0.0 copy-start.2
  19.1 95.2 %all_to_all.10 = bf16[8,80,3072]{2,1,0:T(8,128)(2,1)} all-to-all(bf16[8,80,3072]{2,1,0:T(8,128)(2,1)S(1)} %bitcast.41), channel_id=1, replica_groups=mesh['dp'=4,'expert'=8,'etp'=16] {'expert'}, dimensions={0} | all-to-all | bytes 7864320 | tf_op jit(solution)/shard_map/all_to_all | solution.py:30
  114.4 0.0 copy-done
  114.4 0.0 copy-done.2
  114.4 8.2 %convolution_convert_fusion = bf16[640,3072]{1,0:T(8,128)(2,1)} fusion(bf16[1,256,3072]{2,1,0:T(8,128)(2,1)S(1)} %copy-done, bf16[640,3072]{1,0:T(8,128)(2,1)} %bitcast.43, bf16[1,3072,256]{2,1,0:T(8,128)(2,1)S(1)} %copy-done.2), kind=kOutput, calls=%fused_computation.3 | convolution fusion | flops 2016051200 | bytes 11010048 | tf_op jit(solution)/shard_map/dot_general | solution.py:34
  122.5 6.2 %copy.32 = bf16[8,80,3072]{2,0,1:T(8,128)(2,1)} copy(bf16[8,80,3072]{2,1,0:T(8,128)(2,1)} %bitcast.44) | data formatting | bytes 7864320 | tf_op jit(solution)/shard_map/convert_element_type | solution.py:38
  128.7 0.0 copy-start.1
  128.7 0.0 reduce-scatter.2.cloned.1.call-update
  128.7 0.0 all-gather.2.cloned.1.call-start
  128.8 66.1 %reduce-scatter.2.cloned.1.call-done = bf16[8,5,3072]{2,0,1:T(8,128)(2,1)} async-done(((bf16[8,80,3072]{2,0,1:T(8,128)(2,1)}), bf16[8,5,3072]{2,0,1:T(8,128)(2,1)}) %reduce-scatter.2.cloned.1.call-update) | async-done | bytes 245776 | tf_op jit(solution)/shard_map/reduce_scatter | solution.py:37
  194.9 1.1 copy.33
  196.0 16.7 %all_to_all.11 = bf16[8,5,3072]{2,1,0:T(8,128)(2,1)S(1)} all-to-all(bf16[8,5,3072]{2,1,0:T(8,128)(2,1)S(1)} %copy.33), channel_id=1, replica_groups=mesh['dp'=4,'expert'=8,'etp'=16] {'expert'}, dimensions={0} | all-to-all | bytes 491520 | tf_op jit(solution)/shard_map/all_to_all | solution.py:40
  212.8 0.9 copy.34
  213.6 0.0 all-gather.2.cloned.1.call-update
  213.6 0.0 copy-done.1
  213.7 0.1 copy.38
  213.8 45.4 %all-gather.2.cloned.1.call-done = bf16[8,80,3072]{2,0,1:T(8,128)(2,1)} async-done(((bf16[8,5,3072]{2,0,1:T(8,128)(2,1)}), bf16[8,80,3072]{2,0,1:T(8,128)(2,1)}) %all-gather.2.cloned.1.call-update) | async-done | bytes 3932176 | tf_op jit(solution)/shard_map/all_gather | solution.py:43
  259.2 7.5 %copy.35 = f32[8,80,3072]{2,1,0:T(8,128)} copy(bf16[8,80,3072]{2,0,1:T(8,128)(2,1)} %all-gather.2.cloned.1.call-done) | data formatting | bytes 11796480 | tf_op jit(solution)/shard_map/reshape | solution.py:46
  266.7 8.0 %gather_fusion.1 = f32[256,3072]{1,0:T(8,128)} fusion(f32[640,3072]{1,0:T(8,128)} %bitcast.39, s32[1024]{0:T(1024)S(1)} %pad_clamp_fusion), kind=kCustom, calls=%fused_computation.1 | custom fusion | bytes 6292480 | tf_op jit(solution)/shard_map/gather | solution.py:49
  274.7 8.0 %gather_fusion = f32[256,3072]{1,0:T(8,128)} fusion(f32[640,3072]{1,0:T(8,128)} %bitcast.40, s32[1024]{0:T(1024)S(1)} %pad_clamp_fusion.1), kind=kCustom, calls=%fused_computation | custom fusion | bytes 6292480 | tf_op jit(solution)/shard_map/gather | solution.py:49
  282.7 5.1 %add.100 = f32[256,3072]{1,0:T(8,128)} add(f32[256,3072]{1,0:T(8,128)} %gather_fusion, f32[256,3072]{1,0:T(8,128)} %gather_fusion.1) | non-fusion elementwise | flops 786432 | bytes 9437184 | tf_op jit(solution)/shard_map/add | solution.py:49
  287.8 5.1 %add.101 = f32[128,2,3072]{2,1,0:T(2,128)} reshape(f32[256,3072]{1,0:T(8,128)} %add.100) | data formatting | bytes 6291456 | tf_op jit(solution)/shard_map/add | solution.py:49
  292.8 7.3 %multiply_reduce_fusion = bf16[128,3072]{1,0:T(8,128)(2,1)} fusion(f32[128,2,3072]{2,1,0:T(2,128)} %add.101, f32[128,2]{1,0:T(8,128)S(1)} %copy.38), kind=kLoop, calls=%fused_computation.4 | loop fusion | flops 1179648 | bytes 3933184 | tf_op jit(solution)/shard_map/reduce_sum | solution.py:51
  (7 shorter events, 0.1 us)
Async XLA Ops:
  6.5 107.8 %copy-start = (bf16[1,256,3072]{2,1,0:T(8,128)(2,1)S(1)}, bf16[1,256,3072]{2,1,0:T(8,128)(2,1)}, u32[]{:S(2)}) copy-start(bf16[1,256,3072]{2,1,0:T(8,128)(2,1)} %param.9) | copy-start | bytes 4718596
  6.5 188.4 %reduce-scatter.2.cloned.1.call-start = ((), (), s32[]{:S(2)}) async-start(), calls=%async_computation.3 | async-start | bytes 4177920 | tf_op jit(solution)/shard_map/reduce_scatter | solution.py:37
  19.1 95.2 %copy-start.2 = (bf16[1,3072,256]{2,1,0:T(8,128)(2,1)S(1)}, bf16[1,3072,256]{2,1,0:T(8,128)(2,1)}, u32[]{:S(2)}) copy-start(bf16[1,3072,256]{2,1,0:T(8,128)(2,1)} %param.8) | copy-start | bytes 4718596
  128.7 84.9 %copy-start.1 = (f32[128,2]{0,1:T(2,128)S(1)}, f32[128,2]{0,1:T(2,128)}, u32[]{:S(2)}) copy-start(f32[128,2]{0,1:T(2,128)} %param.7) | copy-start | bytes 3076
  128.7 130.5 %all-gather.2.cloned.1.call-start = ((), (), s32[]{:S(2)}) async-start(), calls=%async_computation.4 | async-start | bytes 4177920 | tf_op jit(solution)/shard_map/all_gather | solution.py:43
Sparse Core Ops, SparseCore 0:
  128.9 66.0 reduce-scatter.1
  213.8 45.4 all-gather.1
where the time goes:
time: 308 us; the launch traced here: 307 us
  blocking collectives  112 us (36%)
  waiting for transfers between devices  112 us (36%)
  local copies, waits for them, and re-layouts  47.3 us (15%)
  other arithmetic  14.4 us (5%)
  between operations  13.5 us (4%)
  matrix products  8.18 us (3%)
    all_to_all x1, blocking collectives, on_device(): lax.all_to_all(outgoing, 'expert', split_axis=0, concat_axis=0, tiled=True)  95.2 us
    reduce_scatter x1, waiting for transfers between devices, on_device(): lax.psum_scatter(partial_terms.astype(jnp.bfloat16), 'etp', scatter_dimen...  66.1 us
    all_gather x1, waiting for transfers between devices, on_device(): lax.all_gather(homeward.astype(jnp.bfloat16), 'etp', axis=1, tiled=True)  45.4 us
    all_to_all x1, blocking collectives, on_device(): lax.all_to_all(summed.astype(jnp.bfloat16), 'expert', split_axis=0, conca...  16.7 us
    gather x2, local copies, waits for them, and re-layouts, on_device(): home_rows[(chosen * halves + half_index) * capacity + position]  16 us
    dot_general x1, matrix products, on_device(): term = jnp.dot(hidden, w_second, preferred_element_type=jnp.float32)  8.18 us
    reshape x1, local copies, waits for them, and re-layouts, on_device(): home_rows = gathered.reshape(n_index * capacity, model_width)  7.47 us
    reduce_sum x1, other arithmetic, on_device(): return jnp.sum(weighted, axis=1).astype(jnp.bfloat16)  7.27 us
  transfers between devices with their start and end apart: 2, of which 2 were waited for; matrix products, arithmetic and copies ran while one was open for 0% of the time, Pallas kernels for 0%

commit v1 on v0

--- a/solution.py
+++ b/solution.py
@@ -2,6 +2,19 @@
 import jax.numpy as jnp
 from jax import lax
 from jax.sharding import PartitionSpec as P
+from jax.lax import all_to_all, psum
+
+
+def set_the_hubs(mine, along_axis="etp"):
+    return jnp.concatenate(
+        all_to_all(
+            jnp.stack([mine for _ in range(psum(1, along_axis))], 0),
+            axis_name=along_axis,
+            split_axis=0,
+            concat_axis=0,
+        ),
+        1,
+    )
 
 
 def on_device(tokens, routes, route_weight, w_in, w_out):
@@ -40,9 +53,7 @@
     homeward = lax.all_to_all(
         summed.astype(jnp.bfloat16), "expert", split_axis=0, concat_axis=0, tiled=True
     ).astype(summed.dtype)
-    gathered = lax.all_gather(homeward.astype(jnp.bfloat16), "etp", axis=1, tiled=True).astype(
-        homeward.dtype
-    )
+    gathered = set_the_hubs(homeward.astype(jnp.bfloat16)).astype(homeward.dtype)
     home_rows = gathered.reshape(n_index * capacity, model_width)
     combined = jnp.zeros((tok_rows * 2, model_width), jnp.float32)
     for half_index in range(halves):

time: 308 us -> 379 us (1.23)
  waiting for transfers between devices: 112 us -> 154 us
  local copies, waits for them, and re-layouts: 47.3 us -> 61 us
  starting transfers between devices: 0.04 us -> 11.7 us
    all_to_all x0 -> x1, waiting for transfers between devices: none -> 87.8 us  [set_the_hubs(): all_to_all(jnp.stack([mine for _ in range(psum(1, along_axis))], 0), axis...]
    all_gather x1 -> x0, waiting for transfers between devices: 45.4 us -> none  [on_device(): lax.all_gather(homeward.astype(jnp.bfloat16), 'etp', axis=1, tiled=True)]
    convert_element_type x0 -> x2, local copies, waits for them, and re-layouts: none -> 19.6 us  [on_device(): set_the_hubs(homeward.astype(jnp.bfloat16)).astype(homeward.dtype)]
    all_to_all x0 -> x1, starting transfers between devices: none -> 11.7 us  [set_the_hubs(): all_to_all(jnp.stack([mine for _ in range(psum(1, along_axis))], 0), axis...]
    reshape x1 -> x0, local copies, waits for them, and re-layouts: 7.47 us -> none  [on_device(): home_rows = gathered.reshape(n_index * capacity, model_width)]
where the time goes in v1:
time: 379 us; the launch traced here: 378 us
  waiting for transfers between devices  154 us (41%)
  blocking collectives  112 us (30%)
  local copies, waits for them, and re-layouts  61 us (16%)
  other arithmetic  17.5 us (5%)
  between operations  13.5 us (4%)
  starting transfers between devices  11.7 us (3%)
  matrix products  8.18 us (2%)
    all_to_all x1, blocking collectives, on_device(): lax.all_to_all(outgoing, 'expert', split_axis=0, concat_axis=0, tiled=True)  95.2 us
    all_to_all x1, waiting for transfers between devices, set_the_hubs(): all_to_all(jnp.stack([mine for _ in range(psum(1, along_axis))], 0), axis...  87.8 us
    reduce_scatter x1, waiting for transfers between devices, on_device(): lax.psum_scatter(partial_terms.astype(jnp.bfloat16), 'etp', scatter_dimen...  66.2 us
    convert_element_type x2, local copies, waits for them, and re-layouts, on_device(): set_the_hubs(homeward.astype(jnp.bfloat16)).astype(homeward.dtype)  19.6 us
    all_to_all x1, blocking collectives, on_device(): lax.all_to_all(summed.astype(jnp.bfloat16), 'expert', split_axis=0, conca...  16.7 us
    gather x2, local copies, waits for them, and re-layouts, on_device(): home_rows[(chosen * halves + half_index) * capacity + position]  15.9 us
    all_to_all x1, starting transfers between devices, set_the_hubs(): all_to_all(jnp.stack([mine for _ in range(psum(1, along_axis))], 0), axis...  11.7 us
    dot_general x1, matrix products, on_device(): term = jnp.dot(hidden, w_second, preferred_element_type=jnp.float32)  8.18 us
  transfers between devices with their start and end apart: 2, of which 2 were waited for; matrix products, arithmetic and copies ran while one was open for 0% of the time, Pallas kernels for 0%

profile of v1, /device:TPU:1, one launch (start us, length us, event | category | flops | bytes accessed | tf_op | source)
XLA Modules:
  0.0 377.9 jit_solution(17705078081651748386)
XLA Ops:
  6.5 0.0 copy-start
  6.5 0.0 reduce-scatter.2.cloned.1.call-start
  6.5 0.9 copy.28
  7.4 0.1 eq.29
  7.6 0.1 eq.25
  7.7 0.7 add_multiply_fusion
  8.4 1.2 reduce-window.6
  9.6 0.1 slice.12
  9.7 0.1 copy.30
  9.9 0.1 copy.31
  10.0 0.1 add_bitcast_fusion
  10.0 0.1 copy.27
  10.1 0.1 mul.69
  10.3 0.1 copy.36
  10.4 0.1 mul.74
  10.5 0.1 copy.37
  10.7 0.1 mul.77
  10.8 1.9 broadcast_in_dim.7
  12.8 1.5 reshape.165
  14.3 4.2 %scatter_custom_fusion = bf16[320,3072]{1,0:T(8,128)(2,1)S(1)} fusion(s32[256]{0:T(256)S(1)} %bitcast.48, bf16[256,3072]{1,0:T(8,128)(2,1)} %reshape.165, bf16[]{:T(256)} %constant.5.clone.1), kind=kCustom, calls=%fused_computation.9 | custom fusion | bytes 1966592 | tf_op jit(solution)/shard_map/scatter | solution.py:38
  18.5 0.6 broadcast_in_dim.16
  19.1 0.0 copy-start.3
  19.1 95.2 %all_to_all.15 = bf16[8,80,3072]{2,1,0:T(8,128)(2,1)} all-to-all(bf16[8,80,3072]{2,1,0:T(8,128)(2,1)S(1)} %bitcast.40), channel_id=1, replica_groups=mesh['dp'=4,'expert'=8,'etp'=16] {'expert'}, dimensions={0} | all-to-all | bytes 7864320 | tf_op jit(solution)/shard_map/all_to_all | solution.py:43
  114.4 0.0 copy-done
  114.4 0.0 copy-done.3
  114.4 8.2 %convolution_convert_fusion = bf16[640,3072]{1,0:T(8,128)(2,1)} fusion(bf16[1,256,3072]{2,1,0:T(8,128)(2,1)S(1)} %copy-done, bf16[640,3072]{1,0:T(8,128)(2,1)} %bitcast.42, bf16[1,3072,256]{2,1,0:T(8,128)(2,1)S(1)} %copy-done.3), kind=kOutput, calls=%fused_computation.4 | convolution fusion | flops 2016051200 | bytes 11010048 | tf_op jit(solution)/shard_map/dot_general | solution.py:47
  122.5 6.2 %copy.32 = bf16[8,80,3072]{2,0,1:T(8,128)(2,1)} copy(bf16[8,80,3072]{2,1,0:T(8,128)(2,1)} %bitcast.43) | data formatting | bytes 7864320 | tf_op jit(solution)/shard_map/convert_element_type | solution.py:51
  128.7 0.0 reduce-scatter.2.cloned.1.call-update
  128.7 66.2 %reduce-scatter.2.cloned.1.call-done = bf16[8,5,3072]{2,0,1:T(8,128)(2,1)} async-done(((bf16[8,80,3072]{2,0,1:T(8,128)(2,1)}), bf16[8,5,3072]{2,0,1:T(8,128)(2,1)}) %reduce-scatter.2.cloned.1.call-update) | async-done | bytes 245776 | tf_op jit(solution)/shard_map/reduce_scatter | solution.py:50
  194.9 1.1 copy.33
  196.0 16.7 %all_to_all.16 = bf16[8,5,3072]{2,1,0:T(8,128)(2,1)S(1)} all-to-all(bf16[8,5,3072]{2,1,0:T(8,128)(2,1)S(1)} %copy.33), channel_id=1, replica_groups=mesh['dp'=4,'expert'=8,'etp'=16] {'expert'}, dimensions={0} | all-to-all | bytes 491520 | tf_op jit(solution)/shard_map/all_to_all | solution.py:53
  212.8 0.2 copy.34
  212.9 2.4 stack.2
  215.3 0.0 copy-start.2
  215.3 11.7 %all-to-all-start.2 = ((bf16[16,8,5,3072]{3,1,2,0:T(8,128)(2,1)}), bf16[16,8,5,3072]{3,1,2,0:T(8,128)(2,1)}, u32[]{:S(2)}, u32[]{:S(2)}) async-start(bf16[16,8,5,3072]{3,1,2,0:T(8,128)(2,1)} %stack.2), calls=%async_computation.3 | async-start | bytes 7864320 | tf_op jit(solution)/shard_map/all_to_all | solution.py:10
  227.0 0.0 copy-done.2
  227.0 0.1 copy.38
  227.2 87.8 %all-to-all-done.2 = bf16[16,8,5,3072]{3,1,2,0:T(8,128)(2,1)} async-done(((bf16[16,8,5,3072]{3,1,2,0:T(8,128)(2,1)}), bf16[16,8,5,3072]{3,1,2,0:T(8,128)(2,1)}, u32[]{:S(2)}, u32[]{:S(2)}) %all-to-all-start.2) | async-done | bytes 3932192 | tf_op jit(solution)/shard_map/all_to_all | solution.py:10
  314.9 3.1 convert_bitcast_fusion
  318.1 9.4 %copy.35 = f32[8,16,5,3072]{3,2,1,0:T(8,128)} copy(f32[8,16,5,3072]{3,0,2,1:T(8,128)S(1)} %convert_bitcast_fusion) | data formatting | bytes 15728640 | tf_op jit(solution)/shard_map/convert_element_type | solution.py:56
  327.5 10.1 %reshape.144 = f32[640,3072]{1,0:T(8,128)} reshape(f32[8,16,5,3072]{3,2,1,0:T(8,128)} %copy.35) | data formatting | bytes 15728640 | tf_op jit(solution)/shard_map/convert_element_type | solution.py:56
  337.6 7.9 %gather_fusion.1 = f32[256,3072]{1,0:T(8,128)} fusion(f32[640,3072]{1,0:T(8,128)} %reshape.144, s32[1024]{0:T(1024)S(1)} %pad_clamp_fusion), kind=kCustom, calls=%fused_computation.1 | custom fusion | bytes 6292480 | tf_op jit(solution)/shard_map/gather | solution.py:60
  345.6 7.9 %gather_fusion = f32[256,3072]{1,0:T(8,128)} fusion(f32[640,3072]{1,0:T(8,128)} %reshape.144, s32[1024]{0:T(1024)S(1)} %pad_clamp_fusion.1), kind=kCustom, calls=%fused_computation | custom fusion | bytes 6292480 | tf_op jit(solution)/shard_map/gather | solution.py:60
  353.5 5.0 %add.100 = f32[256,3072]{1,0:T(8,128)} add(f32[256,3072]{1,0:T(8,128)} %gather_fusion, f32[256,3072]{1,0:T(8,128)} %gather_fusion.1) | non-fusion elementwise | flops 786432 | bytes 9437184 | tf_op jit(solution)/shard_map/add | solution.py:60
  358.5 0.0 copy-start.1
  358.6 5.2 %add.101 = f32[128,2,3072]{2,1,0:T(2,128)} reshape(f32[256,3072]{1,0:T(8,128)} %add.100) | data formatting | bytes 6291456 | tf_op jit(solution)/shard_map/add | solution.py:60
  363.7 7.3 %multiply_reduce_fusion = bf16[128,3072]{1,0:T(8,128)(2,1)} fusion(f32[128,2,3072]{2,1,0:T(2,128)} %add.101, f32[128,2]{1,0:T(8,128)S(1)} %copy.38), kind=kLoop, calls=%fused_computation.5 | loop fusion | flops 1179648 | bytes 3933184 | tf_op jit(solution)/shard_map/reduce_sum | solution.py:62
  371.0 0.0 copy-done.1
  (7 shorter events, 0.1 us)
Async XLA Ops:
  6.5 107.8 %copy-start = (bf16[1,256,3072]{2,1,0:T(8,128)(2,1)S(1)}, bf16[1,256,3072]{2,1,0:T(8,128)(2,1)}, u32[]{:S(2)}) copy-start(bf16[1,256,3072]{2,1,0:T(8,128)(2,1)} %param.9) | copy-start | bytes 4718596
  6.5 188.4 %reduce-scatter.2.cloned.1.call-start = ((), (), s32[]{:S(2)}) async-start(), calls=%async_computation.4 | async-start | bytes 4177920 | tf_op jit(solution)/shard_map/reduce_scatter | solution.py:50
  19.1 95.2 %copy-start.3 = (bf16[1,3072,256]{2,1,0:T(8,128)(2,1)S(1)}, bf16[1,3072,256]{2,1,0:T(8,128)(2,1)}, u32[]{:S(2)}) copy-start(bf16[1,3072,256]{2,1,0:T(8,128)(2,1)} %param.8) | copy-start | bytes 4718596
  215.3 11.7 %copy-start.2 = (f32[128,2]{0,1:T(2,128)S(1)}, f32[128,2]{0,1:T(2,128)}, u32[]{:S(2)}) copy-start(f32[128,2]{0,1:T(2,128)} %param.7) | copy-start | bytes 3076
  215.3 99.6 %all-to-all-start.2 = ((bf16[16,8,5,3072]{3,1,2,0:T(8,128)(2,1)}), bf16[16,8,5,3072]{3,1,2,0:T(8,128)(2,1)}, u32[]{:S(2)}, u32[]{:S(2)}) async-start(bf16[16,8,5,3072]{3,1,2,0:T(8,128)(2,1)} %stack.2), calls=%async_computation.3 | async-start | bytes 7864320 | tf_op jit(solution)/shard_map/all_to_all | solution.py:10
  358.5 12.5 %copy-start.1 = (bf16[1,256,3072]{2,1,0:T(8,128)(2,1)S(1)}, bf16[1,256,3072]{2,1,0:T(8,128)(2,1)}, u32[]{:S(2)}) copy-start(bf16[1,256,3072]{2,1,0:T(8,128)(2,1)} %param.9) | copy-start | bytes 4718596
Sparse Core Ops, SparseCore 0:
  128.9 66.0 reduce-scatter.1
